TPU v7x, 32 devices: a whole 2x2x4 slice. The times are simulated.
32 devices in a mesh: illum: 2 (over y), gx: 4 (over x, core), gy: 4 (over z).
Axes of the slice: x: 2, y: 2, z: 4, core: 2. Of those that a mesh axis runs over, the one named last changes fastest.
Arguments:
- density: float32 [128, 64, 128], P('gx', 'gy'), may hold values from 0 to 1
- moment_one: float32 [128, 64, 128], P('gx', 'gy'), may hold values from -0.6 to 0.6
- moment_two: float32 [128, 64, 128], P('gx', 'gy'), may hold values from 0.0002 to 0.0006
- forward_field: bfloat16 [2, 2, 3, 128, 64, 128], P('illum', None, None, 'gx', 'gy'), may hold values from -6 to 6
- adjoint_field: bfloat16 [2, 2, 3, 128, 64, 128], P('illum', None, None, 'gx', 'gy'), may hold values from -6 to 6
- objective_weight: float32 [2], P('illum'), may hold values from 0.02 to 0.2
Outputs:
- new_density: float32 [128, 64, 128], P('gx', 'gy')
- new_moment_one: float32 [128, 64, 128], P('gx', 'gy')
- new_moment_two: float32 [128, 64, 128], P('gx', 'gy')
- physical: float32 [128, 64, 128], P('gx', 'gy')
All inputs are finite; a program needn't handle non-finite values.
Results may differ from a plain program's by a relative error of at most 0.0003.
Values sent between devices are 32-bit elements; how exact they have to be, the bound alone decides.
A program may use at most 64 MiB of HBM per device.

v0:
```python
import jax
import jax.numpy as jnp
from jax import lax
from jax.sharding import PartitionSpec as P

RADIUS = 8


sharpness = 8.0
threshold = 0.5


def extended(value, sides, width):
    for axis, dim in sides:
        size, length = (lax.axis_size(axis), value.shape[dim])
        up = [(i, (i + 1) % size) for i in range(size - 1)]
        down = [(j, i) for i, j in up]
        last = lax.slice_in_dim(value, length - width, length, axis=dim)
        leading = lax.slice_in_dim(value, 0, width, axis=dim)
        before = lax.ppermute(last, axis, up)
        after = lax.ppermute(leading, axis, down)
        value = jnp.concatenate([before, value, after], axis=dim)
    return value


def tap_weights():
    offsets = jnp.arange(-RADIUS, RADIUS + 1)
    return ((RADIUS + 1 - jnp.abs(offsets)) / (RADIUS + 1) ** 2).astype(jnp.float32)


def band_matrix(length):
    rows = jnp.arange(length)[:, None]
    cols = jnp.arange(length)[None, :]
    apart = jnp.abs(rows - cols)
    values = (RADIUS + 1 - apart).astype(jnp.float32) / float((RADIUS + 1) ** 2)
    return jnp.where(apart <= RADIUS, values, jnp.float32(0.0))


def line_filter(padded, axis, length):
    weights = tap_weights()
    total = jnp.zeros(padded.shape[:axis] + (length,) + padded.shape[axis + 1 :], jnp.float32)
    for offset in range(2 * RADIUS + 1):
        total = total + weights[offset] * lax.slice_in_dim(
            padded, offset, offset + length, axis=axis
        )
    return total


def depth_filter(field):
    shape = field.shape
    flat = field.reshape(-1, shape[2])
    out = jnp.dot(
        flat,
        band_matrix(shape[2]),
        precision=lax.Precision.HIGHEST,
        preferred_element_type=jnp.float32,
    )
    return out.reshape(shape)


def tile_filter(field):
    padded_x = extended(field, (("gx", 0),), RADIUS)
    along_x = line_filter(padded_x, 0, field.shape[0])
    padded_y = extended(along_x, (("gy", 1),), RADIUS)
    along_y = line_filter(padded_y, 1, field.shape[1])
    return depth_filter(along_y)


def project(value):
    scale = jnp.tanh(sharpness * threshold) + jnp.tanh(sharpness * (1.0 - threshold))
    return (jnp.tanh(sharpness * threshold) + jnp.tanh(sharpness * (value - threshold))) / scale


def slope(value):
    scale = jnp.tanh(sharpness * threshold) + jnp.tanh(sharpness * (1.0 - threshold))
    inner = jnp.tanh(sharpness * (value - threshold))
    return sharpness * (1.0 - inner * inner) / scale


def shards(density, moment_one, moment_two, forward_field, adjoint_field, objective_weight):
    filtered = tile_filter(density)
    real_part = forward_field[:, 0].astype(jnp.float32) * adjoint_field[:, 0].astype(jnp.float32)
    imag_part = forward_field[:, 1].astype(jnp.float32) * adjoint_field[:, 1].astype(jnp.float32)
    intersection = jnp.sum(real_part - imag_part, axis=1)
    local_term = jnp.einsum("s,sxyz->xyz", objective_weight, intersection)
    sensitivity = lax.psum(local_term, "illum")
    chained = sensitivity * slope(filtered)
    gradient = tile_filter(chained)
    new_moment_one = 0.9 * moment_one + 0.1 * gradient
    new_moment_two = 0.999 * moment_two + 0.001 * gradient * gradient
    first_fix = 1.0 - 0.9**5
    second_fix = 1.0 - 0.999**5
    step = new_moment_one / first_fix / (jnp.sqrt(new_moment_two / second_fix) + 1e-08)
    new_density = jnp.clip(density - 0.05 * step, 0.0, 1.0)
    physical = project(tile_filter(new_density))
    return (new_density, new_moment_one, new_moment_two, physical)


def solution(mesh):
    in_specs = (
        P("gx", "gy", None),
        P("gx", "gy", None),
        P("gx", "gy", None),
        P("illum", None, None, "gx", "gy", None),
        P("illum", None, None, "gx", "gy", None),
        P("illum"),
    )
    out_specs = (P("gx", "gy", None), P("gx", "gy", None), P("gx", "gy", None), P("gx", "gy", None))
    return jax.shard_map(shards, mesh=mesh, in_specs=in_specs, out_specs=out_specs, check_vma=False)
```

profile of v0, /device:TPU:1, one launch (start us, length us, event | category | flops | bytes accessed | tf_op | source)
XLA Modules:
  0.0 143.3 jit_solution(4802256783518562704)
XLA Ops:
  8.1 4.5 %collective-permute-start = (f32[8,16,128]{2,1,0:T(8,128)S(1)}, f32[8,16,128]{2,1,0:T(8,128)S(1)}, u32[]{:S(2)}, u32[]{:S(2)}) collective-permute-start(f32[8,16,128]{2,1,0:T(8,128)S(1)} %get-tuple-element.19), channel_id=1, source_target_pairs={{0,4},{4,8},{8,12},{1,5},{5,9},{9,13},{2,6},{6,10},{10,14},{3,7},{... | collective-permute-start | bytes 196616 | tf_op jit(solution)/shard_map/ppermute | solution.py:20
  12.6 1.9 %collective-permute-start.1 = (f32[8,16,128]{2,1,0:T(8,128)S(1)}, f32[8,16,128]{2,1,0:T(8,128)S(1)}, u32[]{:S(2)}, u32[]{:S(2)}) collective-permute-start(f32[8,16,128]{2,1,0:T(8,128)S(1)} %get-tuple-element.20), channel_id=1, source_target_pairs={{4,0},{8,4},{12,8},{5,1},{9,5},{13,9},{6,2},{10,6},{14,10},{7,3},{... | collective-permute-start | bytes 196616 | tf_op jit(solution)/shard_map/ppermute | solution.py:21
  15.2 1.6 %subtract_reduce_fusion = f32[32,16,128]{2,1,0:T(8,128)S(1)} fusion(bf16[1,2,3,32,16,128]{5,4,3,2,1,0:T(8,128)(2,1)} %param.10, bf16[1,2,3,32,16,128]{5,4,3,2,1,0:T(8,128)(2,1)} %param.9), kind=kLoop, calls=%fused_computation.82 | loop fusion | flops 1507328 | bytes 1835008 | tf_op jit(solution)/shard_map/reduce_sum | solution.py:84
  18.5 10.7 %fusion.296 = f32[32,16,128]{2,1,0:T(8,128)S(1)} fusion(f32[40,16,128]{2,1,0:T(8,128)S(1)} %constant_dynamic-update-slice_fusion.2, f32[40,16,128]{2,1,0:T(8,128)S(1)} %get-tuple-element.17, f32[32,16,128]{2,1,0:T(8,128)S(1)} %copy-done, f32[]{:T(128)} %bitcast.17, f32[]{:T(128)} %bitcast.16, f32[]{:T(128)} %bitcast.15, f32[]{:T(128)} %bitcast.14, ...), kind=kLoop, calls=%fused_computation.403 | loop fusion | flops 2162688 | bytes 4718660 | tf_op jit(solution)/shard_map/add | solution.py:43
  29.2 3.2 %collective-permute-start.2 = (f32[32,8,128]{2,1,0:T(8,128)S(1)}, f32[32,8,128]{2,1,0:T(8,128)S(1)}, u32[]{:S(2)}, u32[]{:S(2)}) collective-permute-start(f32[32,8,128]{2,1,0:T(8,128)S(1)} %get-tuple-element.15), channel_id=1, source_target_pairs={{0,1},{1,2},{2,3},{4,5},{5,6},{6,7},{8,9},{9,10},{10,11},{12,13},{... | collective-permute-start | bytes 393224 | tf_op jit(solution)/shard_map/ppermute | solution.py:20
  32.4 1.3 collective-permute-start.3
  34.4 4.0 %collective-permute-done.3 = f32[32,8,128]{2,1,0:T(8,128)S(1)} collective-permute-done((f32[32,8,128]{2,1,0:T(8,128)S(1)}, f32[32,8,128]{2,1,0:T(8,128)S(1)}, u32[]{:S(2)}, u32[]{:S(2)}) %collective-permute-start.3) | collective-permute-done | bytes 131104 | tf_op jit(solution)/shard_map/ppermute | solution.py:21
  38.4 3.3 %all-reduce.2.cloned.1.call-done = f32[32,16,128]{2,1,0:T(8,128)} async-done(((f32[32,16,128]{2,1,0:T(8,128)}), f32[32,16,128]{2,1,0:T(8,128)}) %all-reduce.2.cloned.1.call-update) | async-done | bytes 262160 | tf_op jit(solution)/shard_map/psum | solution.py:86
  41.7 12.4 %fusion.8 = f32[32,16,128]{2,1,0:T(8,128)S(1)} fusion(f32[32,16,128]{2,1,0:T(8,128)} %all-reduce.2.cloned.1.call-done, f32[32,16,128]{2,1,0:T(8,128)S(1)} %fusion.296, f32[32,8,128]{2,1,0:T(8,128)S(1)} %collective-permute-done.3, f32[32,8,128]{2,1,0:T(8,128)S(1)} %collective-permute-done.2, f32[]{:T(128)} %bitcast.17, f32[]{:T(128)} %bitcast.16, ...), kind=kOutput, calls=%fused_computation.10 | convolution fusion | flops 104382464 | bytes 1048644 | tf_op jit(solution)/shard_map/dot_general | solution.py:52
  54.1 4.2 %collective-permute-start.4 = (f32[8,16,128]{2,1,0:T(8,128)S(1)}, f32[8,16,128]{2,1,0:T(8,128)S(1)}, u32[]{:S(2)}, u32[]{:S(2)}) collective-permute-start(f32[8,16,128]{2,1,0:T(8,128)S(1)} %get-tuple-element.13), channel_id=1, source_target_pairs={{0,4},{4,8},{8,12},{1,5},{5,9},{9,13},{2,6},{6,10},{10,14},{3,7},{... | collective-permute-start | bytes 196616 | tf_op jit(solution)/shard_map/ppermute | solution.py:20
  58.3 1.9 %collective-permute-start.5 = (f32[8,16,128]{2,1,0:T(8,128)S(1)}, f32[8,16,128]{2,1,0:T(8,128)S(1)}, u32[]{:S(2)}, u32[]{:S(2)}) collective-permute-start(f32[8,16,128]{2,1,0:T(8,128)S(1)} %get-tuple-element.14), channel_id=1, source_target_pairs={{4,0},{8,4},{12,8},{5,1},{9,5},{13,9},{6,2},{10,6},{14,10},{7,3},{... | collective-permute-start | bytes 196616 | tf_op jit(solution)/shard_map/ppermute | solution.py:21
  60.2 3.6 %collective-permute-done.5 = f32[8,16,128]{2,1,0:T(8,128)S(1)} collective-permute-done((f32[8,16,128]{2,1,0:T(8,128)S(1)}, f32[8,16,128]{2,1,0:T(8,128)S(1)}, u32[]{:S(2)}, u32[]{:S(2)}) %collective-permute-start.5) | collective-permute-done | bytes 65568 | tf_op jit(solution)/shard_map/ppermute | solution.py:21
  63.9 10.7 %fusion.58 = f32[32,16,128]{2,1,0:T(8,128)S(1)} fusion(f32[32,16,128]{2,1,0:T(8,128)S(1)} %fusion.8, f32[8,16,128]{2,1,0:T(8,128)S(1)} %collective-permute-done.5, f32[8,16,128]{2,1,0:T(8,128)S(1)} %collective-permute-done.4, f32[]{:T(128)} %bitcast.17, f32[]{:T(128)} %bitcast.16, f32[]{:T(128)} %bitcast.15, f32[]{:T(128)} %bitcast.14, f32[]{:T(128)} %bitcast.13, ...), kind=kLoop, calls=%fused_computation.202 | loop fusion | flops 3211264 | bytes 655428 | tf_op jit(solution)/shard_map/add | solution.py:43
  74.6 3.2 %collective-permute-start.6 = (f32[32,8,128]{2,1,0:T(8,128)S(1)}, f32[32,8,128]{2,1,0:T(8,128)S(1)}, u32[]{:S(2)}, u32[]{:S(2)}) collective-permute-start(f32[32,8,128]{2,1,0:T(8,128)S(1)} %get-tuple-element.11), channel_id=1, source_target_pairs={{0,1},{1,2},{2,3},{4,5},{5,6},{6,7},{8,9},{9,10},{10,11},{12,13},{... | collective-permute-start | bytes 393224 | tf_op jit(solution)/shard_map/ppermute | solution.py:20
  77.8 1.3 collective-permute-start.7
  79.8 3.8 %collective-permute-done.7 = f32[32,8,128]{2,1,0:T(8,128)S(1)} collective-permute-done((f32[32,8,128]{2,1,0:T(8,128)S(1)}, f32[32,8,128]{2,1,0:T(8,128)S(1)}, u32[]{:S(2)}, u32[]{:S(2)}) %collective-permute-start.7) | collective-permute-done | bytes 131104 | tf_op jit(solution)/shard_map/ppermute | solution.py:21
  83.6 12.4 %subtract_clamp_fusion = (f32[32,16,128]{2,1,0:T(8,128)S(1)}, f32[32,16,128]{2,1,0:T(8,128)}, f32[32,16,128]{2,1,0:T(8,128)}) fusion(f32[32,16,128]{2,1,0:T(8,128)S(1)} %copy-done, f32[32,16,128]{2,1,0:T(8,128)S(1)} %copy-done.2, f32[32,16,128]{2,1,0:T(8,128)S(1)} %copy-done.3, f32[32,16,128]{2,1,0:T(8,128)S(1)} %fusion.58, ...), kind=kOutput, calls=%fused_computation.435 | convolution fusion | flops 104906752 | bytes 2097220 | tf_op jit(solution)/shard_map/dot_general | solution.py:52
  95.9 3.3 %collective-permute-start.8 = (f32[8,16,128]{2,1,0:T(8,128)S(1)}, f32[8,16,128]{2,1,0:T(8,128)S(1)}, u32[]{:S(2)}, u32[]{:S(2)}) collective-permute-start(f32[8,16,128]{2,1,0:T(8,128)S(1)} %get-tuple-element.9), channel_id=1, source_target_pairs={{0,4},{4,8},{8,12},{1,5},{5,9},{9,13},{2,6},{6,10},{10,14},{3,7},{... | collective-permute-start | bytes 196616 | tf_op jit(solution)/shard_map/ppermute | solution.py:20
  99.2 1.9 %collective-permute-start.9 = (f32[8,16,128]{2,1,0:T(8,128)S(1)}, f32[8,16,128]{2,1,0:T(8,128)S(1)}, u32[]{:S(2)}, u32[]{:S(2)}) collective-permute-start(f32[8,16,128]{2,1,0:T(8,128)S(1)} %get-tuple-element.10), channel_id=1, source_target_pairs={{4,0},{8,4},{12,8},{5,1},{9,5},{13,9},{6,2},{10,6},{14,10},{7,3},{... | collective-permute-start | bytes 196616 | tf_op jit(solution)/shard_map/ppermute | solution.py:21
  101.2 3.6 %collective-permute-done.9 = f32[8,16,128]{2,1,0:T(8,128)S(1)} collective-permute-done((f32[8,16,128]{2,1,0:T(8,128)S(1)}, f32[8,16,128]{2,1,0:T(8,128)S(1)}, u32[]{:S(2)}, u32[]{:S(2)}) %collective-permute-start.9) | collective-permute-done | bytes 65568 | tf_op jit(solution)/shard_map/ppermute | solution.py:21
  104.8 10.7 %fusion.14 = f32[32,16,128]{2,1,0:T(8,128)S(1)} fusion(f32[32,16,128]{2,1,0:T(8,128)S(1)} %get-tuple-element.4, f32[8,16,128]{2,1,0:T(8,128)S(1)} %collective-permute-done.9, f32[8,16,128]{2,1,0:T(8,128)S(1)} %collective-permute-done.8, f32[]{:T(128)} %bitcast.17, f32[]{:T(128)} %bitcast.16, f32[]{:T(128)} %bitcast.15, f32[]{:T(128)} %bitcast.14, ...), kind=kLoop, calls=%fused_computation.158 | loop fusion | flops 3211264 | bytes 655428 | tf_op jit(solution)/shard_map/add | solution.py:43
  115.5 3.1 %collective-permute-start.10 = (f32[32,8,128]{2,1,0:T(8,128)S(1)}, f32[32,8,128]{2,1,0:T(8,128)S(1)}, u32[]{:S(2)}, u32[]{:S(2)}) collective-permute-start(f32[32,8,128]{2,1,0:T(8,128)S(1)} %get-tuple-element.7), channel_id=1, source_target_pairs={{0,1},{1,2},{2,3},{4,5},{5,6},{6,7},{8,9},{9,10},{10,11},{12,13},{... | collective-permute-start | bytes 393224 | tf_op jit(solution)/shard_map/ppermute | solution.py:20
  120.6 3.8 %collective-permute-done.11 = f32[32,8,128]{2,1,0:T(8,128)S(1)} collective-permute-done((f32[32,8,128]{2,1,0:T(8,128)S(1)}, f32[32,8,128]{2,1,0:T(8,128)S(1)}, u32[]{:S(2)}, u32[]{:S(2)}) %collective-permute-start.11) | collective-permute-done | bytes 131104 | tf_op jit(solution)/shard_map/ppermute | solution.py:21
  124.4 12.1 %fusion.9 = f32[32,16,128]{2,1,0:T(8,128)} fusion(f32[32,16,128]{2,1,0:T(8,128)S(1)} %fusion.14, f32[32,8,128]{2,1,0:T(8,128)S(1)} %collective-permute-done.11, f32[32,8,128]{2,1,0:T(8,128)S(1)} %collective-permute-done.10, f32[]{:T(128)} %bitcast.17, f32[]{:T(128)} %bitcast.16, f32[]{:T(128)} %bitcast.15, f32[]{:T(128)} %bitcast.14, f32[]{:T(128)} %bitcast.13, ...), kind=kOutput, calls=%fused_computation.11 | convolution fusion | flops 104251392 | bytes 786500 | tf_op jit(solution)/shard_map/dot_general | solution.py:52
  (30 shorter events, 5.9 us)
Async XLA Ops:
  7.2 34.5 %all-reduce.2.cloned.1.call-start = ((), (), s32[]{:S(2)}) async-start(), calls=%async_computation | async-start | bytes 524288 | tf_op jit(solution)/shard_map/psum | solution.py:86
  8.1 10.2 %collective-permute-start = (f32[8,16,128]{2,1,0:T(8,128)S(1)}, f32[8,16,128]{2,1,0:T(8,128)S(1)}, u32[]{:S(2)}, u32[]{:S(2)}) collective-permute-start(f32[8,16,128]{2,1,0:T(8,128)S(1)} %get-tuple-element.19), channel_id=1, source_target_pairs={{0,4},{4,8},{8,12},{1,5},{5,9},{9,13},{2,6},{6,10},{10,14},{3,7},{... | collective-permute-start | bytes 196616 | tf_op jit(solution)/shard_map/ppermute | solution.py:20
  12.6 5.9 %collective-permute-start.1 = (f32[8,16,128]{2,1,0:T(8,128)S(1)}, f32[8,16,128]{2,1,0:T(8,128)S(1)}, u32[]{:S(2)}, u32[]{:S(2)}) collective-permute-start(f32[8,16,128]{2,1,0:T(8,128)S(1)} %get-tuple-element.20), channel_id=1, source_target_pairs={{4,0},{8,4},{12,8},{5,1},{9,5},{13,9},{6,2},{10,6},{14,10},{7,3},{... | collective-permute-start | bytes 196616 | tf_op jit(solution)/shard_map/ppermute | solution.py:21
  17.5 1.0 copy-start
  29.2 5.1 %collective-permute-start.2 = (f32[32,8,128]{2,1,0:T(8,128)S(1)}, f32[32,8,128]{2,1,0:T(8,128)S(1)}, u32[]{:S(2)}, u32[]{:S(2)}) collective-permute-start(f32[32,8,128]{2,1,0:T(8,128)S(1)} %get-tuple-element.15), channel_id=1, source_target_pairs={{0,1},{1,2},{2,3},{4,5},{5,6},{6,7},{8,9},{9,10},{10,11},{12,13},{... | collective-permute-start | bytes 393224 | tf_op jit(solution)/shard_map/ppermute | solution.py:20
  32.4 6.0 %collective-permute-start.3 = (f32[32,8,128]{2,1,0:T(8,128)S(1)}, f32[32,8,128]{2,1,0:T(8,128)S(1)}, u32[]{:S(2)}, u32[]{:S(2)}) collective-permute-start(f32[32,8,128]{2,1,0:T(8,128)S(1)} %get-tuple-element.16), channel_id=1, source_target_pairs={{1,0},{2,1},{3,2},{5,4},{6,5},{7,6},{9,8},{10,9},{11,10},{13,12},{... | collective-permute-start | bytes 393224 | tf_op jit(solution)/shard_map/ppermute | solution.py:21
  54.1 6.1 %collective-permute-start.4 = (f32[8,16,128]{2,1,0:T(8,128)S(1)}, f32[8,16,128]{2,1,0:T(8,128)S(1)}, u32[]{:S(2)}, u32[]{:S(2)}) collective-permute-start(f32[8,16,128]{2,1,0:T(8,128)S(1)} %get-tuple-element.13), channel_id=1, source_target_pairs={{0,4},{4,8},{8,12},{1,5},{5,9},{9,13},{2,6},{6,10},{10,14},{3,7},{... | collective-permute-start | bytes 196616 | tf_op jit(solution)/shard_map/ppermute | solution.py:20
  58.3 5.6 %collective-permute-start.5 = (f32[8,16,128]{2,1,0:T(8,128)S(1)}, f32[8,16,128]{2,1,0:T(8,128)S(1)}, u32[]{:S(2)}, u32[]{:S(2)}) collective-permute-start(f32[8,16,128]{2,1,0:T(8,128)S(1)} %get-tuple-element.14), channel_id=1, source_target_pairs={{4,0},{8,4},{12,8},{5,1},{9,5},{13,9},{6,2},{10,6},{14,10},{7,3},{... | collective-permute-start | bytes 196616 | tf_op jit(solution)/shard_map/ppermute | solution.py:21
  74.5 9.0 %copy-start.2 = (f32[32,16,128]{2,1,0:T(8,128)S(1)}, f32[32,16,128]{2,1,0:T(8,128)}, u32[]{:S(2)}) copy-start(f32[32,16,128]{2,1,0:T(8,128)} %param.7) | copy-start | bytes 786436
  74.5 9.0 %copy-start.3 = (f32[32,16,128]{2,1,0:T(8,128)S(1)}, f32[32,16,128]{2,1,0:T(8,128)}, u32[]{:S(2)}) copy-start(f32[32,16,128]{2,1,0:T(8,128)} %param.8) | copy-start | bytes 786436
  74.6 5.2 %collective-permute-start.6 = (f32[32,8,128]{2,1,0:T(8,128)S(1)}, f32[32,8,128]{2,1,0:T(8,128)S(1)}, u32[]{:S(2)}, u32[]{:S(2)}) collective-permute-start(f32[32,8,128]{2,1,0:T(8,128)S(1)} %get-tuple-element.11), channel_id=1, source_target_pairs={{0,1},{1,2},{2,3},{4,5},{5,6},{6,7},{8,9},{9,10},{10,11},{12,13},{... | collective-permute-start | bytes 393224 | tf_op jit(solution)/shard_map/ppermute | solution.py:20
  77.8 5.7 %collective-permute-start.7 = (f32[32,8,128]{2,1,0:T(8,128)S(1)}, f32[32,8,128]{2,1,0:T(8,128)S(1)}, u32[]{:S(2)}, u32[]{:S(2)}) collective-permute-start(f32[32,8,128]{2,1,0:T(8,128)S(1)} %get-tuple-element.12), channel_id=1, source_target_pairs={{1,0},{2,1},{3,2},{5,4},{6,5},{7,6},{9,8},{10,9},{11,10},{13,12},{... | collective-permute-start | bytes 393224 | tf_op jit(solution)/shard_map/ppermute | solution.py:21
  95.9 19.6 %copy-start.1 = (f32[32,16,128]{2,1,0:T(8,128)}, f32[32,16,128]{2,1,0:T(8,128)S(1)}, u32[]{:S(2)}) copy-start(f32[32,16,128]{2,1,0:T(8,128)S(1)} %get-tuple-element.4) | copy-start | bytes 786436
  95.9 5.2 %collective-permute-start.8 = (f32[8,16,128]{2,1,0:T(8,128)S(1)}, f32[8,16,128]{2,1,0:T(8,128)S(1)}, u32[]{:S(2)}, u32[]{:S(2)}) collective-permute-start(f32[8,16,128]{2,1,0:T(8,128)S(1)} %get-tuple-element.9), channel_id=1, source_target_pairs={{0,4},{4,8},{8,12},{1,5},{5,9},{9,13},{2,6},{6,10},{10,14},{3,7},{... | collective-permute-start | bytes 196616 | tf_op jit(solution)/shard_map/ppermute | solution.py:20
  99.2 5.6 %collective-permute-start.9 = (f32[8,16,128]{2,1,0:T(8,128)S(1)}, f32[8,16,128]{2,1,0:T(8,128)S(1)}, u32[]{:S(2)}, u32[]{:S(2)}) collective-permute-start(f32[8,16,128]{2,1,0:T(8,128)S(1)} %get-tuple-element.10), channel_id=1, source_target_pairs={{4,0},{8,4},{12,8},{5,1},{9,5},{13,9},{6,2},{10,6},{14,10},{7,3},{... | collective-permute-start | bytes 196616 | tf_op jit(solution)/shard_map/ppermute | solution.py:21
  115.5 5.0 %collective-permute-start.10 = (f32[32,8,128]{2,1,0:T(8,128)S(1)}, f32[32,8,128]{2,1,0:T(8,128)S(1)}, u32[]{:S(2)}, u32[]{:S(2)}) collective-permute-start(f32[32,8,128]{2,1,0:T(8,128)S(1)} %get-tuple-element.7), channel_id=1, source_target_pairs={{0,1},{1,2},{2,3},{4,5},{5,6},{6,7},{8,9},{9,10},{10,11},{12,13},{... | collective-permute-start | bytes 393224 | tf_op jit(solution)/shard_map/ppermute | solution.py:20
  118.7 5.7 %collective-permute-start.11 = (f32[32,8,128]{2,1,0:T(8,128)S(1)}, f32[32,8,128]{2,1,0:T(8,128)S(1)}, u32[]{:S(2)}, u32[]{:S(2)}) collective-permute-start(f32[32,8,128]{2,1,0:T(8,128)S(1)} %get-tuple-element.8), channel_id=1, source_target_pairs={{1,0},{2,1},{3,2},{5,4},{6,5},{7,6},{9,8},{10,9},{11,10},{13,12},{... | collective-permute-start | bytes 393224 | tf_op jit(solution)/shard_map/ppermute | solution.py:21
Sparse Core Ops, SparseCore 0:
  17.6 23.9 all-reduce.1
where the time goes:
time: 145 us; the launch traced here: 143 us
  matrix products  36.9 us (25%)
  other arithmetic  34.4 us (24%)
  starting transfers between devices  31.2 us (22%)
  waiting for transfers between devices  24.1 us (17%)
  between operations  14.9 us (10%)
  local copies, waits for them, and re-layouts  1.93 us (1%)
    dot_general x3, matrix products, depth_filter(): jnp.dot(flat, band_matrix(shape[2]), precision=lax.Precision.HIGHEST, pre...  36.9 us
    add x3, other arithmetic, line_filter(): total + weights[offset] * lax.slice_in_dim(padded, offset, offset + lengt...  32 us
    ppermute x6, starting transfers between devices, extended(): before = lax.ppermute(last, axis, up)  21.5 us
    ppermute x6, waiting for transfers between devices, extended(): after = lax.ppermute(leading, axis, down)  18.9 us
    ppermute x6, starting transfers between devices, extended(): after = lax.ppermute(leading, axis, down)  9.64 us
    psum x1, waiting for transfers between devices, shards(): sensitivity = lax.psum(local_term, 'illum')  3.28 us
  transfers between devices with their start and end apart: 13, of which 9 were waited for; matrix products, arithmetic and copies ran while one was open for 10% of the time, Pallas kernels for 0%

commit v1 on v0

v1 whole, which is shorter than its diff:
```python
import functools
import math

import jax
import jax.numpy as jnp
from jax import lax
from jax.experimental import pallas as pl
from jax.experimental.pallas import tpu as pltpu
from jax.sharding import PartitionSpec as P

RADIUS = 8
SHARPNESS = 8.0
THRESHOLD = 0.5
TANH_EDGE = math.tanh(SHARPNESS * THRESHOLD)
SCALE = math.tanh(SHARPNESS * THRESHOLD) + math.tanh(SHARPNESS * (1.0 - THRESHOLD))
NORM = 1.0 / float((RADIUS + 1) ** 6)
FIRST_FIX = 1.0 / (1.0 - 0.9**5)
SECOND_FIX = 1.0 / (1.0 - 0.999**5)
MESH = pl.DeviceIdType.MESH
ROUNDS = 3


def split(value):
    high = value.astype(jnp.bfloat16)
    low = (value - high.astype(jnp.float32)).astype(jnp.bfloat16)
    return high, low


def box(value):
    n = value.shape[0]
    two = value[: n - 1] + value[1:]
    four = two[: n - 3] + two[2:]
    eight = four[: n - 7] + four[4:]
    return eight[: n - 8] + value[8:]


def plane_matrix(tile_y, group):
    rows, cols = group * tile_y, group * (tile_y + 2 * RADIUS)
    row = lax.broadcasted_iota(jnp.int32, (rows, cols), 0)
    col = lax.broadcasted_iota(jnp.int32, (rows, cols), 1)
    padded = tile_y + 2 * RADIUS
    plane = row // tile_y
    apart = jnp.abs((col - plane * padded) - (row - plane * tile_y) - RADIUS)
    taps = jnp.maximum(RADIUS + 1 - apart, 0)
    return taps.astype(jnp.float32).astype(jnp.bfloat16)


def depth_matrix(length):
    row = lax.broadcasted_iota(jnp.int32, (2 * length, length), 0)
    col = lax.broadcasted_iota(jnp.int32, (2 * length, length), 1)
    row = jnp.where(row >= length, row - length, row)
    taps = jnp.maximum(RADIUS + 1 - jnp.abs(row - col), 0)
    return taps.astype(jnp.float32).astype(jnp.bfloat16)


def kernel(
    sizes,
    den,
    m1,
    m2,
    fwd,
    adj,
    weight,
    new_den,
    new_m1,
    new_m2,
    physical,
    ybuf,
    xbuf,
    sens,
    fbuf,
    abuf,
    m1buf,
    m2buf,
    dbuf,
    pbuf,
    filt,
    local_sem,
    out_sem,
    y_send,
    y_recv,
    x_send,
    x_recv,
    s_send,
    s_recv,
):
    n_illum, n_gx, n_gy = sizes
    tile_x, tile_y, depth = den.shape
    sources, _, comps = fwd.shape[:3]
    me = lax.axis_index("illum")
    gx = lax.axis_index("gx")
    gy = lax.axis_index("gy")
    pieces = [(0, RADIUS), (tile_x - RADIUS, RADIUS), (RADIUS, tile_x - 2 * RADIUS)]
    own = pl.ds(RADIUS, tile_y)

    loads = {}

    def load(name, src, dst):
        copy = pltpu.make_async_copy(src, dst, local_sem.at[len(loads)])
        copy.start()
        loads[name] = copy

    for i, (p, n) in enumerate(pieces):
        part = pl.ds(p, n)
        load(("f", i), fwd.at[:, :, :, part], fbuf.at[:, :, :, part])
        load(("a", i), adj.at[:, :, :, part], abuf.at[:, :, :, part])
    load("d", den, ybuf.at[0, :, own])
    load("m1", m1, m1buf)
    load("m2", m2, m2buf)

    x_prev = (gx > 0, {"gx": jnp.maximum(gx - 1, 0)})
    x_next = (gx < n_gx - 1, {"gx": jnp.minimum(gx + 1, n_gx - 1)})
    y_prev = (gy > 0, {"gy": jnp.maximum(gy - 1, 0)})
    y_next = (gy < n_gy - 1, {"gy": jnp.minimum(gy + 1, n_gy - 1)})
    others = [{"illum": lax.rem(me + k, n_illum)} for k in range(1, n_illum)]

    barrier = pltpu.get_barrier_semaphore()
    for there, device in (y_prev, y_next, x_prev, x_next):

        @pl.when(there)
        def _(device=device):
            pl.semaphore_signal(barrier, inc=1, device_id=device, device_id_type=MESH)

    for device in others:
        pl.semaphore_signal(barrier, inc=1, device_id=device, device_id_type=MESH)
    peers = jnp.int32(len(others))
    for there, _ in (y_prev, y_next, x_prev, x_next):
        peers = peers + there.astype(jnp.int32)
    pl.semaphore_wait(barrier, peers)

    def y_copy(r, d, i, source=None):
        p, n = pieces[i]
        part = pl.ds(p, n)
        if d == 0:
            rows, land, device = RADIUS, RADIUS + tile_y, y_prev[1]
        else:
            rows, land, device = tile_y, 0, y_next[1]
        if source is None:
            src = ybuf.at[r, part, pl.ds(rows, RADIUS)]
        else:
            src = source.at[part, pl.ds(rows - RADIUS, RADIUS)]
        return pltpu.make_async_remote_copy(
            src_ref=src,
            dst_ref=ybuf.at[r, part, pl.ds(land, RADIUS)],
            send_sem=y_send.at[r, d, i],
            recv_sem=y_recv.at[r, d, i],
            device_id=device,
            device_id_type=MESH,
        )

    def x_copy(r, d):
        if d == 0:
            start, land, device = RADIUS, RADIUS + tile_x, x_prev[1]
        else:
            start, land, device = tile_x, 0, x_next[1]
        return pltpu.make_async_remote_copy(
            src_ref=xbuf.at[r, pl.ds(start, RADIUS)],
            dst_ref=xbuf.at[r, pl.ds(land, RADIUS)],
            send_sem=x_send.at[r, d],
            recv_sem=x_recv.at[r, d],
            device_id=device,
            device_id_type=MESH,
        )

    def s_copy(k, i):
        part = pl.ds(*pieces[i])
        return pltpu.make_async_remote_copy(
            src_ref=sens.at[me, part],
            dst_ref=sens.at[me, part],
            send_sem=s_send.at[k, i],
            recv_sem=s_recv.at[k, i],
            device_id=others[k],
            device_id_type=MESH,
        )

    def y_start(r, i, source=None):
        for d, (there, _) in enumerate((y_prev, y_next)):

            @pl.when(there)
            def _(d=d):
                y_copy(r, d, i, source).start()

    def y_arrive(r, i):
        for d, (there, _) in enumerate((y_next, y_prev)):

            @pl.when(there)
            def _(d=d):
                y_copy(r, d, i).wait_recv()

    for i in range(len(pieces)):
        y_start(0, i, den)

    for there, land in ((y_prev[0], 0), (y_next[0], RADIUS + tile_y)):

        @pl.when(jnp.logical_not(there))
        def _(land=land):
            for r in range(ROUNDS):
                ybuf[r, :, pl.ds(land, RADIUS)] = jnp.zeros(
                    (tile_x, RADIUS, depth), jnp.float32
                )

    for there, land in ((x_prev[0], 0), (x_next[0], RADIUS + tile_x)):

        @pl.when(jnp.logical_not(there))
        def _(land=land):
            for r in range(ROUNDS):
                xbuf[r, pl.ds(land, RADIUS)] = jnp.zeros(
                    (RADIUS, tile_y, depth), jnp.float32
                )

    group = RADIUS
    y_taps = plane_matrix(tile_y, group)
    z_taps = depth_matrix(depth)

    for i, (p, n) in enumerate(pieces):
        loads["f", i].wait()
        loads["a", i].wait()
        for q in range(p, p + n):
            total = None
            for s in range(sources):
                real, imag = None, None
                for c in range(comps):
                    a = fbuf[s, 0, c, q].astype(jnp.float32) * abuf[s, 0, c, q].astype(
                        jnp.float32
                    )
                    b = fbuf[s, 1, c, q].astype(jnp.float32) * abuf[s, 1, c, q].astype(
                        jnp.float32
                    )
                    real = (a - b) if real is None else real + (a - b)
                term = weight[s] * real
                total = term if total is None else total + term
            sens[me, q] = total
        for k in range(len(others)):
            s_copy(k, i).start()

    def y_filter(r, i):
        p, n = pieces[i]
        for g in range(p, p + n, group):
            value = ybuf[r, pl.ds(g, group)].reshape(
                group * (tile_y + 2 * RADIUS), depth
            )
            high, low = split(value)
            out = jnp.dot(y_taps, high, preferred_element_type=jnp.float32)
            out = out + jnp.dot(y_taps, low, preferred_element_type=jnp.float32)
            xbuf[r, pl.ds(RADIUS + g, group)] = out.reshape(group, tile_y, depth)

    def xz_filter(r, i):
        p, n = pieces[i]
        halves = []
        for h in range(0, tile_y, 8):
            value = xbuf[r, pl.ds(p, n + 2 * RADIUS), pl.ds(h, 8)]
            halves.append(box(box(value)))
        value = jnp.concatenate(halves, axis=1).reshape(n * tile_y, depth)
        both = jnp.concatenate(split(value), axis=1)
        out = jnp.dot(both, z_taps, preferred_element_type=jnp.float32)
        return (out * NORM).reshape(n, tile_y, depth)

    def through_x(r):
        for i in (0, 1):
            y_arrive(r, i)
            y_filter(r, i)
            there = (x_prev, x_next)[i][0]

            @pl.when(there)
            def _(i=i):
                x_copy(r, i).start()

        y_arrive(r, 2)
        y_filter(r, 2)

    def x_arrive(r, i):
        there = (x_prev, x_next)[i][0]

        @pl.when(there)
        def _():
            x_copy(r, 1 - i).wait_recv()

    def chain(i, filtered):
        p, n = pieces[i]
        part = pl.ds(p, n)
        for k in range(len(others)):
            source = lax.rem(me + n_illum - 1 - k, n_illum)
            pltpu.make_async_remote_copy(
                src_ref=sens.at[me, part],
                dst_ref=sens.at[source, part],
                send_sem=s_send.at[k, i],
                recv_sem=s_recv.at[k, i],
                device_id=others[k],
                device_id_type=MESH,
            ).wait_recv()
        total = sens[0, part]
        for e in range(1, n_illum):
            total = total + sens[e, part]
        inner = jnp.tanh(SHARPNESS * (filtered - THRESHOLD))
        ybuf[1, part, own] = total * (
            SHARPNESS * (1.0 - inner * inner) * (1.0 / SCALE)
        )
        y_start(1, i)

    def update(i, gradient):
        part = pl.ds(*pieces[i])
        one = 0.9 * m1buf[part] + 0.1 * gradient
        two = 0.999 * m2buf[part] + 0.001 * gradient * gradient
        m1buf[part] = one
        m2buf[part] = two
        step = one * FIRST_FIX / (jnp.sqrt(two * SECOND_FIX) + 1e-08)
        value = jnp.clip(ybuf[0, part, own] - 0.05 * step, 0.0, 1.0)
        ybuf[2, part, own] = value
        y_start(2, i)

    def finish(i, value):
        part = pl.ds(*pieces[i])
        pbuf[part] = (TANH_EDGE + jnp.tanh(SHARPNESS * (value - THRESHOLD))) * (
            1.0 / SCALE
        )
        pltpu.make_async_copy(pbuf.at[part], physical.at[part], out_sem.at[i]).start()

    loads["d"].wait()
    through_x(0)
    filt[...] = xz_filter(0, 2)
    for i in (0, 1):
        x_arrive(0, i)
        chain(i, xz_filter(0, i))
    chain(2, filt[...])

    loads["m1"].wait()
    loads["m2"].wait()
    through_x(1)
    filt[...] = xz_filter(1, 2)
    for i in (0, 1):
        x_arrive(1, i)
        update(i, xz_filter(1, i))
    update(2, filt[...])
    stores = [
        pltpu.make_async_copy(m1buf, new_m1, out_sem.at[3]),
        pltpu.make_async_copy(m2buf, new_m2, out_sem.at[4]),
        pltpu.make_async_copy(ybuf.at[2, :, own], new_den, out_sem.at[5]),
    ]
    for store in stores:
        store.start()

    through_x(2)
    finish(2, xz_filter(2, 2))
    for i in (0, 1):
        x_arrive(2, i)
        finish(i, xz_filter(2, i))

    for i, piece in enumerate(pieces):
        part = pl.ds(*piece)
        pltpu.make_async_copy(pbuf.at[part], physical.at[part], out_sem.at[i]).wait()
    for store in stores:
        store.wait()
    for i in range(len(pieces)):
        for k in range(len(others)):
            s_copy(k, i).wait_send()
    for d in (0, 1):

        @pl.when((y_prev, y_next)[d][0])
        def _(d=d):
            for r in range(ROUNDS):
                for i in range(len(pieces)):
                    y_copy(r, d, i, den if r == 0 else None).wait_send()

        @pl.when((x_prev, x_next)[d][0])
        def _(d=d):
            for r in range(ROUNDS):
                x_copy(r, d).wait_send()


def shards(sizes, density, moment_one, moment_two, forward_field, adjoint_field, objective_weight):
    tile_x, tile_y, depth = density.shape
    n_illum = sizes[0]
    tile = jax.ShapeDtypeStruct(density.shape, jnp.float32)
    f32 = jnp.float32
    far = max(n_illum - 1, 1)
    return pl.pallas_call(
        functools.partial(kernel, sizes),
        out_shape=(tile,) * 4,
        in_specs=[pl.BlockSpec(memory_space=pl.ANY)] * 5
        + [pl.BlockSpec(memory_space=pltpu.SMEM)],
        out_specs=(pl.BlockSpec(memory_space=pl.ANY),) * 4,
        scratch_shapes=[
            pltpu.VMEM((ROUNDS, tile_x, tile_y + 2 * RADIUS, depth), f32),
            pltpu.VMEM((ROUNDS, tile_x + 2 * RADIUS, tile_y, depth), f32),
            pltpu.VMEM((n_illum, tile_x, tile_y, depth), f32),
            pltpu.VMEM(forward_field.shape, forward_field.dtype),
            pltpu.VMEM(adjoint_field.shape, adjoint_field.dtype),
            pltpu.VMEM(density.shape, f32),
            pltpu.VMEM(density.shape, f32),
            pltpu.VMEM(density.shape, f32),
            pltpu.VMEM(density.shape, f32),
            pltpu.VMEM((tile_x - 2 * RADIUS, tile_y, depth), f32),
            pltpu.SemaphoreType.DMA((9,)),
            pltpu.SemaphoreType.DMA((6,)),
            pltpu.SemaphoreType.DMA((ROUNDS, 2, 3)),
            pltpu.SemaphoreType.DMA((ROUNDS, 2, 3)),
            pltpu.SemaphoreType.DMA((ROUNDS, 2)),
            pltpu.SemaphoreType.DMA((ROUNDS, 2)),
            pltpu.SemaphoreType.DMA((far, 3)),
            pltpu.SemaphoreType.DMA((far, 3)),
        ],
        compiler_params=pltpu.CompilerParams(collective_id=0, has_side_effects=True),
        name="design_update",
    )(density, moment_one, moment_two, forward_field, adjoint_field, objective_weight)


def solution(mesh):
    field = P("illum", None, None, "gx", "gy", None)
    tile = P("gx", "gy", None)
    sizes = (mesh.shape["illum"], mesh.shape["gx"], mesh.shape["gy"])
    return jax.shard_map(
        functools.partial(shards, sizes),
        mesh=mesh,
        in_specs=(tile, tile, tile, field, field, P("illum")),
        out_specs=(tile,) * 4,
        check_vma=False,
    )
```

time: 145 us -> 30.8 us (0.21)
  matrix products: 36.9 us -> 0 us
  other arithmetic: 34.4 us -> 0 us
  starting transfers between devices: 31.2 us -> 0 us
  Pallas kernels: 0 us -> 24.8 us
  waiting for transfers between devices: 24.1 us -> 0 us
  between operations: 14.9 us -> 1.3 us
  local copies, waits for them, and re-layouts: 1.93 us -> 4.5 us
    dot_general x3 -> x0, matrix products: 36.9 us -> none  [depth_filter(): jnp.dot(flat, band_matrix(shape[2]), precision=lax.Precision.HIGHEST, pre...]
    add x3 -> x0, other arithmetic: 32 us -> none  [line_filter(): total + weights[offset] * lax.slice_in_dim(padded, offset, offset + lengt...]
    ppermute x12 -> x0, starting transfers between devices: 31.2 us -> none  [the longest x6 21.5 us: extended(): before = lax.ppermute(last, axis, up)]
    pallas_call x0 -> x1, Pallas kernels: none -> 24.8 us  [shards(): pl.pallas_call(functools.partial(kernel, sizes), out_shape=(tile,) * 4, i...]
    ppermute x12 -> x0, waiting for transfers between devices: 20.8 us -> none  [the longest x6 18.9 us: extended(): after = lax.ppermute(leading, axis, down)]
    unnamed x9 -> x10, local copies, waits for them, and re-layouts: 0.21 us -> 4.5 us
    psum x1 -> x0, waiting for transfers between devices: 3.28 us -> none  [shards(): sensitivity = lax.psum(local_term, 'illum')]
    slice x7 -> x0, local copies, waits for them, and re-layouts: 1.68 us -> none  [the longest x6 0.96 us: extended(): last = lax.slice_in_dim(value, length - width, length, axis=dim)]
  transfers between devices with their start and end apart: 13 -> 0, of which waited for: 9 -> 0; matrix products, arithmetic and copies ran while one was open for 10% -> 0% of each run, Pallas kernels for 0% -> 0%
where the time goes in v1:
time: 30.8 us; the launch traced here: 30.6 us
  Pallas kernels  24.8 us (81%)
  local copies, waits for them, and re-layouts  4.5 us (15%)
  between operations  1.3 us (4%)
    pallas_call x1, Pallas kernels, shards(): pl.pallas_call(functools.partial(kernel, sizes), out_shape=(tile,) * 4, i...  24.8 us
    unnamed x10, local copies, waits for them, and re-layouts  4.5 us

profile of v1, /device:TPU:1, one launch (start us, length us, event | category | flops | bytes accessed | tf_op | source)
XLA Modules:
  0.0 30.6 jit_solution(7442750415435991920)
XLA Ops:
  1.3 24.8 %design_update.1 = (f32[32,16,128]{2,1,0:T(8,128)}, f32[32,16,128]{2,1,0:T(8,128)}, f32[32,16,128]{2,1,0:T(8,128)}, f32[32,16,128]{2,1,0:T(8,128)}) custom-call(f32[32,16,128]{2,1,0:T(8,128)} %den.1, f32[32,16,128]{2,1,0:T(8,128)} %m1.1, f32[32,16,128]{2,1,0:T(8,128)} %m2.1, bf16[1,2,3,32,16,128]{5,4,3,2,1,0:T(8,128)(2,1)} %fwd.1, ...), custom_call_target="tpu_custom_call" | custom-call | tf_op jit(solution)/shard_map/design_update/pallas_call | solution.py:376
  26.1 0.0 copy-start.2
  26.1 1.7 %copy.15 = f32[32,16,128]{2,1,0:T(8,128)} copy(f32[32,16,128]{2,1,0:T(8,128)} %get-tuple-element.8) | data formatting | bytes 524288
  27.8 0.0 copy-done.2
  27.8 0.0 copy-start.1
  27.8 0.7 %copy.16 = f32[32,16,128]{2,1,0:T(8,128)} copy(f32[32,16,128]{2,1,0:T(8,128)S(1)} %copy-done.2) | data formatting | bytes 524288
  28.5 0.3 %copy-done.1 = f32[32,16,128]{2,1,0:T(8,128)S(1)} copy-done((f32[32,16,128]{2,1,0:T(8,128)S(1)}, f32[32,16,128]{2,1,0:T(8,128)}, u32[]{:S(2)}) %copy-start.1) | copy-done | bytes 262168
  28.8 0.0 copy-start
  28.8 0.7 %copy.17 = f32[32,16,128]{2,1,0:T(8,128)} copy(f32[32,16,128]{2,1,0:T(8,128)S(1)} %copy-done.1) | data formatting | bytes 524288
  29.5 0.3 %copy-done = f32[32,16,128]{2,1,0:T(8,128)S(1)} copy-done((f32[32,16,128]{2,1,0:T(8,128)S(1)}, f32[32,16,128]{2,1,0:T(8,128)}, u32[]{:S(2)}) %copy-start) | copy-done | bytes 262168
  29.9 0.7 %copy.18 = f32[32,16,128]{2,1,0:T(8,128)} copy(f32[32,16,128]{2,1,0:T(8,128)S(1)} %copy-done) | data formatting | bytes 524288
Async XLA Ops:
  26.1 1.7 %copy-start.2 = (f32[32,16,128]{2,1,0:T(8,128)S(1)}, f32[32,16,128]{2,1,0:T(8,128)}, u32[]{:S(2)}) copy-start(f32[32,16,128]{2,1,0:T(8,128)} %get-tuple-element.9) | copy-start | bytes 786436
  27.8 1.0 %copy-start.1 = (f32[32,16,128]{2,1,0:T(8,128)S(1)}, f32[32,16,128]{2,1,0:T(8,128)}, u32[]{:S(2)}) copy-start(f32[32,16,128]{2,1,0:T(8,128)} %get-tuple-element.10) | copy-start | bytes 786436
  28.8 1.0 %copy-start = (f32[32,16,128]{2,1,0:T(8,128)S(1)}, f32[32,16,128]{2,1,0:T(8,128)}, u32[]{:S(2)}) copy-start(f32[32,16,128]{2,1,0:T(8,128)} %get-tuple-element.11) | copy-start | bytes 786436

commit v2 on v1

--- a/solution.py
+++ b/solution.py
@@ -72,11 +72,9 @@
     abuf,
     m1buf,
     m2buf,
-    dbuf,
-    pbuf,
+    wbuf,
     filt,
     local_sem,
-    out_sem,
     y_send,
     y_recv,
     x_send,
@@ -90,7 +88,13 @@
     me = lax.axis_index("illum")
     gx = lax.axis_index("gx")
     gy = lax.axis_index("gy")
-    pieces = [(0, RADIUS), (tile_x - RADIUS, RADIUS), (RADIUS, tile_x - 2 * RADIUS)]
+    side = (gx < n_gx // 2).astype(jnp.int32)
+    reach = tile_x - RADIUS
+    pieces = [
+        (side * reach, RADIUS),
+        ((1 - side) * reach, RADIUS),
+        (RADIUS, tile_x - 2 * RADIUS),
+    ]
     own = pl.ds(RADIUS, tile_y)
 
     loads = {}
@@ -104,18 +108,22 @@
         part = pl.ds(p, n)
         load(("f", i), fwd.at[:, :, :, part], fbuf.at[:, :, :, part])
         load(("a", i), adj.at[:, :, :, part], abuf.at[:, :, :, part])
+    load("w", weight, wbuf)
     load("d", den, ybuf.at[0, :, own])
     load("m1", m1, m1buf)
     load("m2", m2, m2buf)
 
-    x_prev = (gx > 0, {"gx": jnp.maximum(gx - 1, 0)})
-    x_next = (gx < n_gx - 1, {"gx": jnp.minimum(gx + 1, n_gx - 1)})
+    near, far = gx + 2 * side - 1, gx - 2 * side + 1
+    x_sides = [
+        (jnp.logical_and(at >= 0, at < n_gx), {"gx": jnp.clip(at, 0, n_gx - 1)})
+        for at in (near, far)
+    ]
     y_prev = (gy > 0, {"gy": jnp.maximum(gy - 1, 0)})
     y_next = (gy < n_gy - 1, {"gy": jnp.minimum(gy + 1, n_gy - 1)})
     others = [{"illum": lax.rem(me + k, n_illum)} for k in range(1, n_illum)]
 
     barrier = pltpu.get_barrier_semaphore()
-    for there, device in (y_prev, y_next, x_prev, x_next):
+    for there, device in (y_prev, y_next, *x_sides):
 
         @pl.when(there)
         def _(device=device):
@@ -123,8 +131,30 @@
 
     for device in others:
         pl.semaphore_signal(barrier, inc=1, device_id=device, device_id_type=MESH)
+    for there, land in ((y_prev[0], 0), (y_next[0], RADIUS + tile_y)):
+
+        @pl.when(jnp.logical_not(there))
+        def _(land=land):
+            for r in range(ROUNDS):
+                ybuf[r, :, pl.ds(land, RADIUS)] = jnp.zeros(
+                    (tile_x, RADIUS, depth), jnp.float32
+                )
+
+    for there, land in ((gx > 0, 0), (gx < n_gx - 1, RADIUS + tile_x)):
+
+        @pl.when(jnp.logical_not(there))
+        def _(land=land):
+            for r in range(ROUNDS):
+                xbuf[r, pl.ds(land, RADIUS)] = jnp.zeros(
+                    (RADIUS, tile_y, depth), jnp.float32
+                )
+
+    group = RADIUS
+    y_taps = plane_matrix(tile_y, group)
+    z_taps = depth_matrix(depth)
+
     peers = jnp.int32(len(others))
-    for there, _ in (y_prev, y_next, x_prev, x_next):
+    for there, _ in (y_prev, y_next, *x_sides):
         peers = peers + there.astype(jnp.int32)
     pl.semaphore_wait(barrier, peers)
 
@@ -148,17 +178,20 @@
             device_id_type=MESH,
         )
 
-    def x_copy(r, d):
-        if d == 0:
-            start, land, device = RADIUS, RADIUS + tile_x, x_prev[1]
+    def x_copy(r, i, back=False):
+        start = pieces[i][0]
+        high = side if i == 0 else 1 - side
+        if back:
+            land = high * (tile_x + RADIUS)
         else:
-            start, land, device = tile_x, 0, x_next[1]
+            land = (1 - high) * (tile_x + RADIUS)
+        sent, got = (1 - high, high)
         return pltpu.make_async_remote_copy(
-            src_ref=xbuf.at[r, pl.ds(start, RADIUS)],
+            src_ref=xbuf.at[r, pl.ds(RADIUS + start, RADIUS)],
             dst_ref=xbuf.at[r, pl.ds(land, RADIUS)],
-            send_sem=x_send.at[r, d],
-            recv_sem=x_recv.at[r, d],
-            device_id=device,
+            send_sem=x_send.at[r, i],
+            recv_sem=x_recv.at[r, got if back else sent],
+            device_id=x_sides[i][1],
             device_id_type=MESH,
         )
 
@@ -190,32 +223,12 @@
     for i in range(len(pieces)):
         y_start(0, i, den)
 
-    for there, land in ((y_prev[0], 0), (y_next[0], RADIUS + tile_y)):
-
-        @pl.when(jnp.logical_not(there))
-        def _(land=land):
-            for r in range(ROUNDS):
-                ybuf[r, :, pl.ds(land, RADIUS)] = jnp.zeros(
-                    (tile_x, RADIUS, depth), jnp.float32
-                )
-
-    for there, land in ((x_prev[0], 0), (x_next[0], RADIUS + tile_x)):
-
-        @pl.when(jnp.logical_not(there))
-        def _(land=land):
-            for r in range(ROUNDS):
-                xbuf[r, pl.ds(land, RADIUS)] = jnp.zeros(
-                    (RADIUS, tile_y, depth), jnp.float32
-                )
-
-    group = RADIUS
-    y_taps = plane_matrix(tile_y, group)
-    z_taps = depth_matrix(depth)
+    loads["w"].wait()
 
     for i, (p, n) in enumerate(pieces):
         loads["f", i].wait()
         loads["a", i].wait()
-        for q in range(p, p + n):
+        for q in [p + j for j in range(n)]:
             total = None
             for s in range(sources):
                 real, imag = None, None
@@ -227,7 +240,7 @@
                         jnp.float32
                     )
                     real = (a - b) if real is None else real + (a - b)
-                term = weight[s] * real
+                term = wbuf[s] * real
                 total = term if total is None else total + term
             sens[me, q] = total
         for k in range(len(others)):
@@ -235,7 +248,7 @@
 
     def y_filter(r, i):
         p, n = pieces[i]
-        for g in range(p, p + n, group):
+        for g in [p + j for j in range(0, n, group)]:
             value = ybuf[r, pl.ds(g, group)].reshape(
                 group * (tile_y + 2 * RADIUS), depth
             )
@@ -259,7 +272,7 @@
         for i in (0, 1):
             y_arrive(r, i)
             y_filter(r, i)
-            there = (x_prev, x_next)[i][0]
+            there = x_sides[i][0]
 
             @pl.when(there)
             def _(i=i):
@@ -269,11 +282,11 @@
         y_filter(r, 2)
 
     def x_arrive(r, i):
-        there = (x_prev, x_next)[i][0]
+        there = x_sides[i][0]
 
         @pl.when(there)
         def _():
-            x_copy(r, 1 - i).wait_recv()
+            x_copy(r, i, back=True).wait_recv()
 
     def chain(i, filtered):
         p, n = pieces[i]
@@ -301,19 +314,19 @@
         part = pl.ds(*pieces[i])
         one = 0.9 * m1buf[part] + 0.1 * gradient
         two = 0.999 * m2buf[part] + 0.001 * gradient * gradient
-        m1buf[part] = one
-        m2buf[part] = two
+        new_m1[part] = one
+        new_m2[part] = two
         step = one * FIRST_FIX / (jnp.sqrt(two * SECOND_FIX) + 1e-08)
         value = jnp.clip(ybuf[0, part, own] - 0.05 * step, 0.0, 1.0)
         ybuf[2, part, own] = value
         y_start(2, i)
+        new_den[part] = value
 
     def finish(i, value):
         part = pl.ds(*pieces[i])
-        pbuf[part] = (TANH_EDGE + jnp.tanh(SHARPNESS * (value - THRESHOLD))) * (
+        physical[part] = (TANH_EDGE + jnp.tanh(SHARPNESS * (value - THRESHOLD))) * (
             1.0 / SCALE
         )
-        pltpu.make_async_copy(pbuf.at[part], physical.at[part], out_sem.at[i]).start()
 
     loads["d"].wait()
     through_x(0)
@@ -331,25 +344,12 @@
         x_arrive(1, i)
         update(i, xz_filter(1, i))
     update(2, filt[...])
-    stores = [
-        pltpu.make_async_copy(m1buf, new_m1, out_sem.at[3]),
-        pltpu.make_async_copy(m2buf, new_m2, out_sem.at[4]),
-        pltpu.make_async_copy(ybuf.at[2, :, own], new_den, out_sem.at[5]),
-    ]
-    for store in stores:
-        store.start()
-
     through_x(2)
     finish(2, xz_filter(2, 2))
     for i in (0, 1):
         x_arrive(2, i)
         finish(i, xz_filter(2, i))
 
-    for i, piece in enumerate(pieces):
-        part = pl.ds(*piece)
-        pltpu.make_async_copy(pbuf.at[part], physical.at[part], out_sem.at[i]).wait()
-    for store in stores:
-        store.wait()
     for i in range(len(pieces)):
         for k in range(len(others)):
             s_copy(k, i).wait_send()
@@ -361,10 +361,23 @@
                 for i in range(len(pieces)):
                     y_copy(r, d, i, den if r == 0 else None).wait_send()
 
-        @pl.when((x_prev, x_next)[d][0])
+        @pl.when(x_sides[d][0])
         def _(d=d):
             for r in range(ROUNDS):
                 x_copy(r, d).wait_send()
+
+
+def export(a, b, c, d, a_out, b_out, c_out, d_out, sem):
+    copies = [
+        pltpu.make_async_copy(src, dst, sem.at[i])
+        for i, (src, dst) in enumerate(
+            ((a, a_out), (b, b_out), (c, c_out), (d, d_out))
+        )
+    ]
+    for copy in copies:
+        copy.start()
+    for copy in copies:
+        copy.wait()
 
 
 def shards(sizes, density, moment_one, moment_two, forward_field, adjoint_field, objective_weight):
@@ -373,12 +386,11 @@
     tile = jax.ShapeDtypeStruct(density.shape, jnp.float32)
     f32 = jnp.float32
     far = max(n_illum - 1, 1)
-    return pl.pallas_call(
+    results = pl.pallas_call(
         functools.partial(kernel, sizes),
-        out_shape=(tile,) * 4,
-        in_specs=[pl.BlockSpec(memory_space=pl.ANY)] * 5
-        + [pl.BlockSpec(memory_space=pltpu.SMEM)],
-        out_specs=(pl.BlockSpec(memory_space=pl.ANY),) * 4,
+        out_shape=(pltpu.VMEM(density.shape, f32),) * 4,
+        in_specs=[pl.BlockSpec(memory_space=pltpu.HBM)] * 6,
+        out_specs=(pl.BlockSpec(memory_space=pltpu.VMEM),) * 4,
         scratch_shapes=[
             pltpu.VMEM((ROUNDS, tile_x, tile_y + 2 * RADIUS, depth), f32),
             pltpu.VMEM((ROUNDS, tile_x + 2 * RADIUS, tile_y, depth), f32),
@@ -387,11 +399,9 @@
             pltpu.VMEM(adjoint_field.shape, adjoint_field.dtype),
             pltpu.VMEM(density.shape, f32),
             pltpu.VMEM(density.shape, f32),
-            pltpu.VMEM(density.shape, f32),
-            pltpu.VMEM(density.shape, f32),
+            pltpu.SMEM(objective_weight.shape, f32),
             pltpu.VMEM((tile_x - 2 * RADIUS, tile_y, depth), f32),
-            pltpu.SemaphoreType.DMA((9,)),
-            pltpu.SemaphoreType.DMA((6,)),
+            pltpu.SemaphoreType.DMA((10,)),
             pltpu.SemaphoreType.DMA((ROUNDS, 2, 3)),
             pltpu.SemaphoreType.DMA((ROUNDS, 2, 3)),
             pltpu.SemaphoreType.DMA((ROUNDS, 2)),
@@ -399,9 +409,20 @@
             pltpu.SemaphoreType.DMA((far, 3)),
             pltpu.SemaphoreType.DMA((far, 3)),
         ],
-        compiler_params=pltpu.CompilerParams(collective_id=0, has_side_effects=True),
+        compiler_params=pltpu.CompilerParams(
+            collective_id=0, has_side_effects=True, vmem_limit_bytes=48 << 20
+        ),
         name="design_update",
     )(density, moment_one, moment_two, forward_field, adjoint_field, objective_weight)
+    return pl.pallas_call(
+        export,
+        out_shape=(tile,) * 4,
+        in_specs=[pl.BlockSpec(memory_space=pltpu.VMEM)] * 4,
+        out_specs=(pl.BlockSpec(memory_space=pl.ANY),) * 4,
+        scratch_shapes=[pltpu.SemaphoreType.DMA((4,))],
+        compiler_params=pltpu.CompilerParams(vmem_limit_bytes=4 << 20),
+        name="export_results",
+    )(*results)
 
 
 def solution(mesh):

time: 30.8 us -> 32.1 us (1.042)
  local copies, waits for them, and re-layouts: 4.5 us -> 5.11 us
  Pallas kernels: 24.8 us -> 25.3 us
    unnamed x10, local copies, waits for them, and re-layouts: 4.5 us -> 5.11 us
    pallas_call x1 -> x2, Pallas kernels: 24.8 us -> 25.3 us  [the longest x1 24.3 us: shards(): pl.pallas_call(functools.partial(kernel, sizes), out_shape=(pltpu.VMEM(de...]
where the time goes in v2:
time: 32.1 us; the launch traced here: 31.8 us
  Pallas kernels  25.3 us (79%)
  local copies, waits for them, and re-layouts  5.11 us (16%)
  between operations  1.3 us (4%)
    pallas_call x1, Pallas kernels, shards(): pl.pallas_call(functools.partial(kernel, sizes), out_shape=(pltpu.VMEM(de...  24.3 us
    unnamed x10, local copies, waits for them, and re-layouts  5.11 us
    pallas_call x1, Pallas kernels, shards(): pl.pallas_call(export, out_shape=(tile,) * 4, in_specs=[pl.BlockSpec(memo...  1 us

profile of v2, /device:TPU:1, one launch (start us, length us, event | category | flops | bytes accessed | tf_op | source)
XLA Modules:
  0.0 31.8 jit_solution(13141725822974106357)
XLA Ops:
  1.3 0.0 copy-start
  1.3 1.1 %copy-done = bf16[1,2,3,32,16,128]{5,4,3,2,1,0:T(8,128)(2,1)S(1)} copy-done((bf16[1,2,3,32,16,128]{5,4,3,2,1,0:T(8,128)(2,1)S(1)}, bf16[1,2,3,32,16,128]{5,4,3,2,1,0:T(8,128)(2,1)}, u32[]{:S(2)}) %copy-start) | copy-done | bytes 786456
  2.4 0.0 copy-start.1
  2.4 1.1 %copy-done.1 = bf16[1,2,3,32,16,128]{5,4,3,2,1,0:T(8,128)(2,1)S(1)} copy-done((bf16[1,2,3,32,16,128]{5,4,3,2,1,0:T(8,128)(2,1)S(1)}, bf16[1,2,3,32,16,128]{5,4,3,2,1,0:T(8,128)(2,1)}, u32[]{:S(2)}) %copy-start.1) | copy-done | bytes 786456
  3.5 0.0 copy-start.2
  3.5 0.9 %copy-done.2 = f32[32,16,128]{2,1,0:T(8,128)S(1)} copy-done((f32[32,16,128]{2,1,0:T(8,128)S(1)}, f32[32,16,128]{2,1,0:T(8,128)}, u32[]{:S(2)}) %copy-start.2) | copy-done | bytes 262168
  4.5 0.0 copy-start.3
  4.5 0.9 %copy-done.3 = f32[32,16,128]{2,1,0:T(8,128)S(1)} copy-done((f32[32,16,128]{2,1,0:T(8,128)S(1)}, f32[32,16,128]{2,1,0:T(8,128)}, u32[]{:S(2)}) %copy-start.3) | copy-done | bytes 262168
  5.4 0.0 copy-start.4
  5.5 0.9 %copy-done.4 = f32[32,16,128]{2,1,0:T(8,128)S(1)} copy-done((f32[32,16,128]{2,1,0:T(8,128)S(1)}, f32[32,16,128]{2,1,0:T(8,128)}, u32[]{:S(2)}) %copy-start.4) | copy-done | bytes 262168
  6.4 24.3 %design_update.1 = (f32[32,16,128]{2,1,0:T(8,128)S(1)}, f32[32,16,128]{2,1,0:T(8,128)S(1)}, f32[32,16,128]{2,1,0:T(8,128)S(1)}, f32[32,16,128]{2,1,0:T(8,128)S(1)}) custom-call(f32[32,16,128]{2,1,0:T(8,128)S(1)} %copy-done.2, f32[32,16,128]{2,1,0:T(8,128)S(1)} %copy-done.3, f32[32,16,128]{2,1,0:T(8,128)S(1)} %copy-done.4, ...), custom_call_target="tpu_custom_call" | custom-call | tf_op jit(solution)/shard_map/design_update/pallas_call | solution.py:389
  30.8 1.0 %export_results.1 = (f32[32,16,128]{2,1,0:T(8,128)}, f32[32,16,128]{2,1,0:T(8,128)}, f32[32,16,128]{2,1,0:T(8,128)}, f32[32,16,128]{2,1,0:T(8,128)}) custom-call(f32[32,16,128]{2,1,0:T(8,128)S(1)} %get-tuple-element.8.a, f32[32,16,128]{2,1,0:T(8,128)S(1)} %get-tuple-element.9.b, f32[32,16,128]{2,1,0:T(8,128)S(1)} %get-tuple-element.10.c, ...), custom_call_target="tpu_custom_call" | custom-call | tf_op jit(solution)/shard_map/export_results/pallas_call | solution.py:417
Async XLA Ops:
  1.3 1.1 %copy-start = (bf16[1,2,3,32,16,128]{5,4,3,2,1,0:T(8,128)(2,1)S(1)}, bf16[1,2,3,32,16,128]{5,4,3,2,1,0:T(8,128)(2,1)}, u32[]{:S(2)}) copy-start(bf16[1,2,3,32,16,128]{5,4,3,2,1,0:T(8,128)(2,1)} %fwd.1) | copy-start | bytes 2359300
  2.4 1.1 %copy-start.1 = (bf16[1,2,3,32,16,128]{5,4,3,2,1,0:T(8,128)(2,1)S(1)}, bf16[1,2,3,32,16,128]{5,4,3,2,1,0:T(8,128)(2,1)}, u32[]{:S(2)}) copy-start(bf16[1,2,3,32,16,128]{5,4,3,2,1,0:T(8,128)(2,1)} %adj.1) | copy-start | bytes 2359300
  3.5 0.9 %copy-start.2 = (f32[32,16,128]{2,1,0:T(8,128)S(1)}, f32[32,16,128]{2,1,0:T(8,128)}, u32[]{:S(2)}) copy-start(f32[32,16,128]{2,1,0:T(8,128)} %den.1) | copy-start | bytes 786436
  4.5 0.9 %copy-start.3 = (f32[32,16,128]{2,1,0:T(8,128)S(1)}, f32[32,16,128]{2,1,0:T(8,128)}, u32[]{:S(2)}) copy-start(f32[32,16,128]{2,1,0:T(8,128)} %m1.1) | copy-start | bytes 786436
  5.4 0.9 %copy-start.4 = (f32[32,16,128]{2,1,0:T(8,128)S(1)}, f32[32,16,128]{2,1,0:T(8,128)}, u32[]{:S(2)}) copy-start(f32[32,16,128]{2,1,0:T(8,128)} %m2.1) | copy-start | bytes 786436

commit v3 on v2

--- a/solution.py
+++ b/solution.py
@@ -72,7 +72,6 @@
     abuf,
     m1buf,
     m2buf,
-    wbuf,
     filt,
     local_sem,
     y_send,
@@ -108,7 +107,6 @@
         part = pl.ds(p, n)
         load(("f", i), fwd.at[:, :, :, part], fbuf.at[:, :, :, part])
         load(("a", i), adj.at[:, :, :, part], abuf.at[:, :, :, part])
-    load("w", weight, wbuf)
     load("d", den, ybuf.at[0, :, own])
     load("m1", m1, m1buf)
     load("m2", m2, m2buf)
@@ -223,8 +221,6 @@
     for i in range(len(pieces)):
         y_start(0, i, den)
 
-    loads["w"].wait()
-
     for i, (p, n) in enumerate(pieces):
         loads["f", i].wait()
         loads["a", i].wait()
@@ -240,7 +236,7 @@
                         jnp.float32
                     )
                     real = (a - b) if real is None else real + (a - b)
-                term = wbuf[s] * real
+                term = weight[s] * real
                 total = term if total is None else total + term
             sens[me, q] = total
         for k in range(len(others)):
@@ -386,10 +382,15 @@
     tile = jax.ShapeDtypeStruct(density.shape, jnp.float32)
     f32 = jnp.float32
     far = max(n_illum - 1, 1)
+    arguments = [
+        pltpu.with_memory_space_constraint(x, pltpu.HBM)
+        for x in (density, moment_one, moment_two, forward_field, adjoint_field)
+    ]
     results = pl.pallas_call(
         functools.partial(kernel, sizes),
         out_shape=(pltpu.VMEM(density.shape, f32),) * 4,
-        in_specs=[pl.BlockSpec(memory_space=pltpu.HBM)] * 6,
+        in_specs=[pl.BlockSpec(memory_space=pltpu.HBM)] * 5
+        + [pl.BlockSpec(memory_space=pltpu.SMEM)],
         out_specs=(pl.BlockSpec(memory_space=pltpu.VMEM),) * 4,
         scratch_shapes=[
             pltpu.VMEM((ROUNDS, tile_x, tile_y + 2 * RADIUS, depth), f32),
@@ -399,9 +400,8 @@
             pltpu.VMEM(adjoint_field.shape, adjoint_field.dtype),
             pltpu.VMEM(density.shape, f32),
             pltpu.VMEM(density.shape, f32),
-            pltpu.SMEM(objective_weight.shape, f32),
             pltpu.VMEM((tile_x - 2 * RADIUS, tile_y, depth), f32),
-            pltpu.SemaphoreType.DMA((10,)),
+            pltpu.SemaphoreType.DMA((9,)),
             pltpu.SemaphoreType.DMA((ROUNDS, 2, 3)),
             pltpu.SemaphoreType.DMA((ROUNDS, 2, 3)),
             pltpu.SemaphoreType.DMA((ROUNDS, 2)),
@@ -413,7 +413,7 @@
             collective_id=0, has_side_effects=True, vmem_limit_bytes=48 << 20
         ),
         name="design_update",
-    )(density, moment_one, moment_two, forward_field, adjoint_field, objective_weight)
+    )(*arguments, objective_weight)
     return pl.pallas_call(
         export,
         out_shape=(tile,) * 4,

time: 32.1 us -> 26.7 us (0.83)
  local copies, waits for them, and re-layouts: 5.11 us -> 0 us
    unnamed x10 -> x0, local copies, waits for them, and re-layouts: 5.11 us -> none
where the time goes in v3:
time: 26.7 us; the launch traced here: 26.6 us
  Pallas kernels  25.3 us (95%)
  between operations  1.29 us (5%)
    pallas_call x1, Pallas kernels, shards(): pl.pallas_call(functools.partial(kernel, sizes), out_shape=(pltpu.VMEM(de...  24.3 us
    pallas_call x1, Pallas kernels, shards(): pl.pallas_call(export, out_shape=(tile,) * 4, in_specs=[pl.BlockSpec(memo...  1 us

profile of v3, /device:TPU:1, one launch (start us, length us, event | category | flops | bytes accessed | tf_op | source)
XLA Modules:
  0.0 26.6 jit_solution(1804666293679449387)
XLA Ops:
  1.3 24.3 %design_update.1 = (f32[32,16,128]{2,1,0:T(8,128)S(1)}, f32[32,16,128]{2,1,0:T(8,128)S(1)}, f32[32,16,128]{2,1,0:T(8,128)S(1)}, f32[32,16,128]{2,1,0:T(8,128)S(1)}) custom-call(f32[32,16,128]{2,1,0:T(8,128)} %den.1, f32[32,16,128]{2,1,0:T(8,128)} %m1.1, f32[32,16,128]{2,1,0:T(8,128)} %m2.1, bf16[1,2,3,32,16,128]{5,4,3,2,1,0:T(8,128)(2,1)} %fwd.1, ...), custom_call_target="tpu_custom_call" | custom-call | tf_op jit(solution)/shard_map/design_update/pallas_call | solution.py:389
  25.6 1.0 %export_results.1 = (f32[32,16,128]{2,1,0:T(8,128)}, f32[32,16,128]{2,1,0:T(8,128)}, f32[32,16,128]{2,1,0:T(8,128)}, f32[32,16,128]{2,1,0:T(8,128)}) custom-call(f32[32,16,128]{2,1,0:T(8,128)S(1)} %get-tuple-element.8.a, f32[32,16,128]{2,1,0:T(8,128)S(1)} %get-tuple-element.9.b, f32[32,16,128]{2,1,0:T(8,128)S(1)} %get-tuple-element.10.c, ...), custom_call_target="tpu_custom_call" | custom-call | tf_op jit(solution)/shard_map/export_results/pallas_call | solution.py:417

commit v4 on v3

--- a/solution.py
+++ b/solution.py
@@ -32,17 +32,6 @@
     four = two[: n - 3] + two[2:]
     eight = four[: n - 7] + four[4:]
     return eight[: n - 8] + value[8:]
-
-
-def plane_matrix(tile_y, group):
-    rows, cols = group * tile_y, group * (tile_y + 2 * RADIUS)
-    row = lax.broadcasted_iota(jnp.int32, (rows, cols), 0)
-    col = lax.broadcasted_iota(jnp.int32, (rows, cols), 1)
-    padded = tile_y + 2 * RADIUS
-    plane = row // tile_y
-    apart = jnp.abs((col - plane * padded) - (row - plane * tile_y) - RADIUS)
-    taps = jnp.maximum(RADIUS + 1 - apart, 0)
-    return taps.astype(jnp.float32).astype(jnp.bfloat16)
 
 
 def depth_matrix(length):
@@ -148,7 +137,6 @@
                 )
 
     group = RADIUS
-    y_taps = plane_matrix(tile_y, group)
     z_taps = depth_matrix(depth)
 
     peers = jnp.int32(len(others))
@@ -245,13 +233,16 @@
     def y_filter(r, i):
         p, n = pieces[i]
         for g in [p + j for j in range(0, n, group)]:
-            value = ybuf[r, pl.ds(g, group)].reshape(
-                group * (tile_y + 2 * RADIUS), depth
-            )
-            high, low = split(value)
-            out = jnp.dot(y_taps, high, preferred_element_type=jnp.float32)
-            out = out + jnp.dot(y_taps, low, preferred_element_type=jnp.float32)
-            xbuf[r, pl.ds(RADIUS + g, group)] = out.reshape(group, tile_y, depth)
+            total = None
+            for k in range(RADIUS + 1):
+                row = ybuf[r, pl.ds(g, group), pl.ds(k, tile_y)]
+                if k < RADIUS:
+                    row = row + ybuf[
+                        r, pl.ds(g, group), pl.ds(2 * RADIUS - k, tile_y)
+                    ]
+                row = row * float(k + 1)
+                total = row if total is None else total + row
+            xbuf[r, pl.ds(RADIUS + g, group)] = total
 
     def xz_filter(r, i):
         p, n = pieces[i]

time: 26.7 us -> 26.4 us (0.989)
  Pallas kernels: 25.3 us -> 24.9 us
    pallas_call x1, Pallas kernels: 24.3 us -> 23.9 us  [shards(): pl.pallas_call(functools.partial(kernel, sizes), out_shape=(pltpu.VMEM(de...]
where the time goes in v4:
time: 26.4 us; the launch traced here: 26.2 us
  Pallas kernels  24.9 us (94%)
  between operations  1.29 us (5%)
    pallas_call x1, Pallas kernels, shards(): pl.pallas_call(functools.partial(kernel, sizes), out_shape=(pltpu.VMEM(de...  23.9 us
    pallas_call x1, Pallas kernels, shards(): pl.pallas_call(export, out_shape=(tile,) * 4, in_specs=[pl.BlockSpec(memo...  1 us

profile of v4, /device:TPU:1, one launch (start us, length us, event | category | flops | bytes accessed | tf_op | source)
XLA Modules:
  0.0 26.2 jit_solution(9507173800218423170)
XLA Ops:
  1.3 23.9 %design_update.1 = (f32[32,16,128]{2,1,0:T(8,128)S(1)}, f32[32,16,128]{2,1,0:T(8,128)S(1)}, f32[32,16,128]{2,1,0:T(8,128)S(1)}, f32[32,16,128]{2,1,0:T(8,128)S(1)}) custom-call(f32[32,16,128]{2,1,0:T(8,128)} %den.1, f32[32,16,128]{2,1,0:T(8,128)} %m1.1, f32[32,16,128]{2,1,0:T(8,128)} %m2.1, bf16[1,2,3,32,16,128]{5,4,3,2,1,0:T(8,128)(2,1)} %fwd.1, ...), custom_call_target="tpu_custom_call" | custom-call | tf_op jit(solution)/shard_map/design_update/pallas_call | solution.py:380
  25.2 1.0 %export_results.1 = (f32[32,16,128]{2,1,0:T(8,128)}, f32[32,16,128]{2,1,0:T(8,128)}, f32[32,16,128]{2,1,0:T(8,128)}, f32[32,16,128]{2,1,0:T(8,128)}) custom-call(f32[32,16,128]{2,1,0:T(8,128)S(1)} %get-tuple-element.8.a, f32[32,16,128]{2,1,0:T(8,128)S(1)} %get-tuple-element.9.b, f32[32,16,128]{2,1,0:T(8,128)S(1)} %get-tuple-element.10.c, ...), custom_call_target="tpu_custom_call" | custom-call | tf_op jit(solution)/shard_map/export_results/pallas_call | solution.py:408

commit v5 on v4

--- a/solution.py
+++ b/solution.py
@@ -333,7 +333,7 @@
     update(2, filt[...])
     through_x(2)
     finish(2, xz_filter(2, 2))
-    for i in (0, 1):
+    for i in (1, 0):
         x_arrive(2, i)
         finish(i, xz_filter(2, i))
 

time: 26.4 us -> 26.2 us (level)
  no operation moved by 1% of the time
where the time goes in v5:
time: 26.2 us; the launch traced here: 26 us
  Pallas kernels  24.7 us (94%)
  between operations  1.29 us (5%)
    pallas_call x1, Pallas kernels, shards(): pl.pallas_call(functools.partial(kernel, sizes), out_shape=(pltpu.VMEM(de...  23.7 us
    pallas_call x1, Pallas kernels, shards(): pl.pallas_call(export, out_shape=(tile,) * 4, in_specs=[pl.BlockSpec(memo...  1 us

profile of v5, /device:TPU:1, one launch (start us, length us, event | category | flops | bytes accessed | tf_op | source)
XLA Modules:
  0.0 26.0 jit_solution(11244860966653901488)
XLA Ops:
  1.3 23.7 %design_update.1 = (f32[32,16,128]{2,1,0:T(8,128)S(1)}, f32[32,16,128]{2,1,0:T(8,128)S(1)}, f32[32,16,128]{2,1,0:T(8,128)S(1)}, f32[32,16,128]{2,1,0:T(8,128)S(1)}) custom-call(f32[32,16,128]{2,1,0:T(8,128)} %den.1, f32[32,16,128]{2,1,0:T(8,128)} %m1.1, f32[32,16,128]{2,1,0:T(8,128)} %m2.1, bf16[1,2,3,32,16,128]{5,4,3,2,1,0:T(8,128)(2,1)} %fwd.1, ...), custom_call_target="tpu_custom_call" | custom-call | tf_op jit(solution)/shard_map/design_update/pallas_call | solution.py:380
  25.0 1.0 %export_results.1 = (f32[32,16,128]{2,1,0:T(8,128)}, f32[32,16,128]{2,1,0:T(8,128)}, f32[32,16,128]{2,1,0:T(8,128)}, f32[32,16,128]{2,1,0:T(8,128)}) custom-call(f32[32,16,128]{2,1,0:T(8,128)S(1)} %get-tuple-element.8.a, f32[32,16,128]{2,1,0:T(8,128)S(1)} %get-tuple-element.9.b, f32[32,16,128]{2,1,0:T(8,128)S(1)} %get-tuple-element.10.c, ...), custom_call_target="tpu_custom_call" | custom-call | tf_op jit(solution)/shard_map/export_results/pallas_call | solution.py:408
